TPU v7x, 32 devices: a whole 2x2x4 slice. The times are simulated.
32 devices in a mesh: dp: 4 (over y, core), item: 8 (over z, x).
Axes of the slice: x: 2, y: 2, z: 4, core: 2. Of those that a mesh axis runs over, the one named last changes fastest.
Arguments:
- query: bfloat16 [32, 256], P(('dp', 'item')), may hold values from -40 to 40
- item_table: bfloat16 [65536, 256], P(('dp', 'item')), may hold values from -2.5 to 2.5
- context_features: bfloat16 [32, 512], P(('dp', 'item')), may hold values from -6 to 6
- candidates: int32 [32, 1024], P(('dp', 'item')), may hold values from 0 to 65535, as said below
- lengths: int32 [32], P(('dp', 'item')), may hold values from 128 to 1024, as said below
- logged_slot: int32 [32], P(('dp', 'item')), may hold values from 0 to 1023, as said below
- logging_prop: int32 [32], P(('dp', 'item')), may hold values from 256 to 4095
- w_first: bfloat16 [768, 512], replicated, may hold values from -0.21875 to 0.21875
- w_second: bfloat16 [512, 512], replicated, may hold values from -0.25 to 0.25
- w_score: bfloat16 [512], replicated, may hold values from -0.5 to 0.5
Outputs:
- section_logp: float32 [32, 1024], P(('dp', 'item'))
- log_weight: float32 [32], P(('dp', 'item'))
Inputs may be any that keep to these rules, and one draw needn't show every extreme that they name: `candidates`: item ids. Among the 1024 candidate slots held by one device (its single context), at most 48 name items of any one block of 2048 consecutive ids, and for every device some block is named exactly 48 times. `lengths`: some context's list has 1024 live slots and some context's list has 128. `logged_slot`: below the context's length; the context with the longest list logs its last slot.
All inputs are finite; a program needn't handle non-finite values.
Results may differ from a plain program's by a relative error of at most 0.0003.
Values may be sent and summed in bfloat16 or wider, within the bound.
A program may use at most 64 MiB of HBM per device.

v0:
```python
import functools
import math

import jax
import jax.numpy as jnp
from jax import lax
from jax.experimental import pallas as pl
from jax.experimental.pallas import tpu as pltpu
from jax.sharding import PartitionSpec as P

F32 = jnp.float32
BF16 = jnp.bfloat16
LANES = 128
NT = (((1,), (1,)), ((), ()))
NN = (((1,), (0,)), ((), ()))
TN = (((0,), (0,)), ((), ()))


def round_up(value, step):
    return (value + step - 1) // step * step


def dot(left, right, dims):
    return lax.dot_general(left, right, dims, preferred_element_type=F32)


def silu(v):
    half = v * 0.5
    return half + half * jnp.tanh(half)


def kernel(
    dp_size,
    item_size,
    groups,
    cap,
    query_hbm,
    feature_hbm,
    cand_hbm,
    scalar_hbm,
    table_hbm,
    first_hbm,
    second_hbm,
    score_hbm,
    section_ref,
    weight_ref,
    query_ref,
    feature_ref,
    cand_ref,
    scalar_ref,
    score_ref,
    table,
    first,
    second_w,
    send1,
    recv1,
    send2,
    recv2,
    load_sem,
    send_sem,
    arrive_sem,
    return_sem,
    own_sem,
    items,
    found,
    wanted_v,
    wanted_at,
    index_sem,
):
    n = dp_size * item_size
    item_rows, width = table.shape
    slots = cand_ref.shape[1]
    feature_width = feature_ref.shape[1]
    hidden_width = first.shape[1]
    gen_at = round_up(cap, 8)
    max_at = 2 * gen_at
    dp_me, item_me = lax.axis_index("dp"), lax.axis_index("item")
    me = dp_me * item_size + item_me
    run = item_size // groups
    members = dp_size * run
    run_me = lax.div(item_me, run)
    member_me = dp_me * run + lax.rem(item_me, run)

    def device(offset, member):
        dp = lax.div(member, run)
        item = lax.rem(run_me + offset, groups) * run + lax.rem(member, run)
        return dp * item_size + item, {"dp": dp, "item": item}

    def each_peer(offset, act):
        @pl.loop(1 if offset == 0 else 0, members)
        def visit(j):
            member = lax.rem(member_me + j, members)
            peer, where = device(offset, member)
            act(member, peer, where)

    barrier = pltpu.get_barrier_semaphore()

    def greet(member, peer, where):
        pl.semaphore_signal(barrier, inc=1, device_id=where, device_id_type=pl.DeviceIdType.MESH)

    far_first = sorted(range(groups), key=lambda g: -min(g, groups - g))
    for offset in far_first:
        each_peer(offset, greet)

    loads = [
        pltpu.make_async_copy(source, target, load_sem.at[i])
        for i, (source, target) in enumerate(
            [
                (cand_hbm, cand_ref),
                (query_hbm, query_ref),
                (feature_hbm, feature_ref),
                (first_hbm, first),
                (table_hbm, table),
                (second_hbm, second_w),
                (score_hbm, score_ref),
                (scalar_hbm, scalar_ref),
            ]
        )
    ]
    for load in loads:
        load.start()
    loads[0].wait()

    ids = cand_ref[...]
    holder = lax.div(ids, item_rows)
    local = ids - holder * item_rows
    high = lax.div(local, LANES).astype(F32)
    low = lax.rem(local, LANES).astype(F32)
    held = (lax.broadcasted_iota(jnp.int32, (n, slots), 0) == holder).astype(F32)
    blocks = slots // LANES
    stacked = jnp.concatenate(
        [held[:, b * LANES : (b + 1) * LANES] for b in range(blocks)], axis=0
    ).astype(BF16)
    before = (
        lax.broadcasted_iota(jnp.int32, (LANES, LANES), 0)
        < lax.broadcasted_iota(jnp.int32, (LANES, LANES), 1)
    ).astype(F32)
    counter = jnp.concatenate([before, jnp.ones((LANES, LANES), F32)], axis=1).astype(BF16)
    counts = dot(stacked, counter, NN)
    total = jnp.zeros((n, LANES), F32)
    rank_parts = []
    for b in range(blocks):
        here = counts[b * n : (b + 1) * n]
        place = here[:, :LANES] + total
        rank_parts.append(
            jnp.sum(held[:, b * LANES : (b + 1) * LANES] * place, axis=0, keepdims=True)
        )
        total = total + here[:, LANES:]
    rank = jnp.concatenate(rank_parts, axis=1)
    at_rank = (
        lax.broadcasted_iota(jnp.int32, (LANES, slots), 0).astype(F32) == rank
    ).astype(F32)
    parts = jnp.concatenate([held * high, held * low], axis=0).astype(BF16)
    asked = dot(parts, at_rank.astype(BF16), NT)
    asked = asked[:n] * float(LANES) + asked[n:]

    for load in loads[1:4]:
        load.wait()
    context_part = dot(feature_ref[...], first[:feature_width, :], NN)
    send1[:, 0, :width] = jnp.broadcast_to(query_ref[...].astype(F32), (n, width))
    send1[:, 0, width : width + hidden_width] = jnp.broadcast_to(context_part, (n, hidden_width))
    send1[:, 0, width + hidden_width :] = asked

    pl.semaphore_wait(barrier, n - 1)

    def ask(offset):
        seen = (groups - offset) % groups

        def act(member, peer, where):
            pltpu.make_async_remote_copy(
                src_ref=send1.at[pl.ds(peer, 1)],
                dst_ref=recv1.at[pl.ds(seen * members + member_me, 1)],
                send_sem=send_sem.at[0],
                recv_sem=arrive_sem.at[seen],
                device_id=where,
                device_id_type=pl.DeviceIdType.MESH,
            ).start()

        each_peer(offset, act)

    def give_back(offset):
        def act(member, peer, where):
            pltpu.make_async_remote_copy(
                src_ref=send2.at[pl.ds(offset * members + member, 1)],
                dst_ref=recv2.at[pl.ds(me, 1)],
                send_sem=send_sem.at[1],
                recv_sem=return_sem,
                device_id=where,
                device_id_type=pl.DeviceIdType.MESH,
            ).start()

        each_peer(offset, act)

    def wait_rows(buffer, count, semaphore):
        rows = buffer.at[pl.ds(0, count)]
        pltpu.make_async_copy(rows, rows, semaphore).wait()

    own_ask = pltpu.make_async_copy(
        send1.at[pl.ds(me, 1)], recv1.at[pl.ds(member_me, 1)], own_sem.at[0]
    )
    own_ask.start()
    for offset in far_first:
        ask(offset)
    for load in loads[4:]:
        load.wait()
    own_ask.wait()

    lane = lax.broadcasted_iota(jnp.int32, (members, LANES), 1)
    score_rows = jnp.broadcast_to(score_ref[...].reshape(1, hidden_width), (LANES, hidden_width))
    hidden_tiles = hidden_width // LANES
    tall = items.shape[1]
    step = math.gcd(256, item_rows)

    @pl.loop(0, item_rows // step)
    def project(i):
        part = pl.ds(pl.multiple_of(i * step, step), step)
        block = table[part]
        projected = dot(block, first[feature_width:, :], NN)
        for j in range(hidden_tiles):
            items[part, j] = projected[:, j * LANES : (j + 1) * LANES]
        for j in range(width // LANES):
            items[part, hidden_tiles + j] = block[:, j * LANES : (j + 1) * LANES].astype(F32)


    def to_scalar(group):
        rows_here = pl.ds(group * members, members)
        return pltpu.make_async_copy(
            wanted_v.at[rows_here], wanted_at.at[rows_here], index_sem.at[group]
        )

    def rank_group(group):
        rows_here = pl.ds(group * members, members)
        query = recv1[rows_here, 0, :width]
        context = recv1[rows_here, 0, width : width + hidden_width]
        to_scalar(group).wait()
        for r in range(cap):
            for c in range(members):
                at = jnp.clip(wanted_at[group * members + c, 0, r], 0, item_rows - 1)
                place = (group * cap + r) * members + c
                found[pl.ds(place * tall, tall)] = items[at]
        count = cap * members

        def found_tile(j):
            return found[pl.ds(group * count * tall + j, count, stride=tall), :]

        item_part = jnp.concatenate([found_tile(j) for j in range(hidden_tiles)], axis=1)
        rows = jnp.concatenate(
            [found_tile(hidden_tiles + j) for j in range(width // LANES)], axis=1
        )
        hidden = silu(item_part + jnp.concatenate([context] * cap, axis=0)).astype(BF16)
        second = silu(dot(hidden, second_w[...], NN)).astype(BF16)
        score = dot(second, score_rows, NT)
        result = jnp.zeros((members, LANES), F32)
        for r in range(cap):
            mine = slice(r * members, (r + 1) * members)
            gen = jnp.sum(rows[mine] * query, axis=1, keepdims=True)
            result = jnp.where(lane == r, score[mine], result)
            result = jnp.where(lane == gen_at + r, gen, result)
        return result

    def normalizers():
        logits = dot(recv1[:, 0, :width].astype(BF16), table[...], NT)
        local_max = jnp.max(logits, axis=1, keepdims=True)
        local_sum = jnp.sum(jnp.exp(logits - local_max), axis=1, keepdims=True)
        return local_max, local_sum

    order = sorted(range(groups), key=lambda g: min(g, groups - g))
    order = order[:-2] + order[:-3:-1]
    results = {}
    waited = set()

    def wait_group(group):
        if group not in waited:
            waited.add(group)
            wait_rows(recv1, members - 1 if group == 0 else members, arrive_sem.at[group])
            rows_here = pl.ds(group * members, members)
            wanted_v[rows_here] = recv1[rows_here, :, width + hidden_width :].astype(jnp.int32)
            to_scalar(group).start()

    for group in order[:-2]:
        wait_group(group)
        results[group] = rank_group(group)
    for group in order[-2:]:
        wait_group(group)
    local_max, local_sum = normalizers()

    def finish(group):
        mine = slice(group * members, (group + 1) * members)
        result = jnp.where(lane == max_at, local_max[mine], results[group])
        result = jnp.where(lane == max_at + 1, local_sum[mine], result)
        send2[pl.ds(group * members, members), 0, :] = result
        give_back(group)

    for group in reversed(order[:-2]):
        finish(group)
    own_back = pltpu.make_async_copy(
        send2.at[pl.ds(member_me, 1)], recv2.at[pl.ds(me, 1)], own_sem.at[1]
    )
    own_back.start()
    for group in order[-2:]:
        results[group] = rank_group(group)
        finish(group)
    own_back.wait()
    wait_rows(send1, n - 1, send_sem.at[0])
    wait_rows(recv2, n - 1, return_sem)

    back = recv2[:, 0, :]
    top = back.astype(BF16)
    rest = back - top.astype(F32)
    middle = rest.astype(BF16)
    bottom = (rest - middle.astype(F32)).astype(BF16)
    pieces = jnp.concatenate([top.astype(F32), middle.astype(F32), bottom.astype(F32)], axis=0)
    held_bf = held.astype(BF16)
    spread = dot(
        pieces.astype(BF16).T, jnp.concatenate([held_bf, held_bf, held_bf], axis=0), NN
    )
    score = jnp.sum(at_rank[:gen_at] * spread[:gen_at], axis=0, keepdims=True)
    gen = jnp.sum(at_rank[:gen_at] * spread[gen_at : 2 * gen_at], axis=0, keepdims=True)

    maxima = back[:, max_at : max_at + 1]
    sums = back[:, max_at + 1 : max_at + 2]
    peak = jnp.max(maxima, axis=0, keepdims=True)
    log_norm = peak + jnp.log(jnp.sum(sums * jnp.exp(maxima - peak), axis=0, keepdims=True))

    length = scalar_ref[:, 0:1]
    position = lax.broadcasted_iota(jnp.int32, (1, slots), 1)
    live = position < length
    masked = jnp.where(live, score, -1e30)
    rank_peak = jnp.max(masked, axis=1, keepdims=True)
    rank_norm = rank_peak + jnp.log(
        jnp.sum(jnp.where(live, jnp.exp(masked - rank_peak), 0.0), axis=1, keepdims=True)
    )
    section = jnp.where(
        live, score - rank_norm + gen - log_norm + math.log(item_rows * n), 0.0
    )
    chosen = jnp.sum(jnp.where(position == scalar_ref[:, 1:2], section, 0.0), axis=1, keepdims=True)
    prop = scalar_ref[:, 2:3].astype(F32) / 1024.0
    section_ref[...] = section
    weight_ref[...] = chosen + jnp.log(length.astype(F32)) - jnp.log(prop)
    wait_rows(send2, n - 1, send_sem.at[1])


def solution(mesh):
    dp_size, item_size = mesh.shape["dp"], mesh.shape["item"]
    n = dp_size * item_size

    def body(
        query,
        item_table,
        context_features,
        candidates,
        lengths,
        logged_slot,
        logging_prop,
        w_first,
        w_second,
        w_score,
    ):
        slots = candidates.shape[1]
        cap = max(2, 3 * slots // (2 * n))
        width = query.shape[1]
        hidden_width = w_first.shape[1]
        message = width + hidden_width + LANES
        tall = round_up((width + hidden_width) // LANES, 8)
        vmem = pl.BlockSpec(memory_space=pltpu.VMEM)
        groups = math.gcd(4, item_size)
        lane = lax.broadcasted_iota(jnp.int32, (1, LANES), 1)
        scalars = jnp.where(lane == 0, lengths, jnp.where(lane == 1, logged_slot, logging_prop))
        section, weight = pl.pallas_call(
            functools.partial(kernel, dp_size, item_size, groups, cap),
            out_shape=(
                pltpu.VMEM((1, slots), F32),
                pltpu.VMEM((1, 1), F32),
            ),
            in_specs=[pl.BlockSpec(memory_space=pltpu.HBM)] * 8,
            out_specs=(vmem, vmem),
            scratch_shapes=[
                pltpu.VMEM(query.shape, BF16),
                pltpu.VMEM(context_features.shape, BF16),
                pltpu.VMEM(candidates.shape, jnp.int32),
                pltpu.VMEM((1, LANES), jnp.int32),
                pltpu.VMEM(w_score.shape, BF16),
                pltpu.VMEM(item_table.shape, BF16),
                pltpu.VMEM(w_first.shape, BF16),
                pltpu.VMEM(w_second.shape, BF16),
                pltpu.VMEM((n, 1, message), F32),
                pltpu.VMEM((n, 1, message), F32),
                pltpu.VMEM((n, 1, LANES), F32),
                pltpu.VMEM((n, 1, LANES), F32),
                pltpu.SemaphoreType.DMA((8,)),
                pltpu.SemaphoreType.DMA((2,)),
                pltpu.SemaphoreType.DMA((groups,)),
                pltpu.SemaphoreType.DMA,
                pltpu.SemaphoreType.DMA((2,)),
                pltpu.VMEM((item_table.shape[0], tall, LANES), F32),
                pltpu.VMEM((n * cap * tall + tall, LANES), F32),
                pltpu.VMEM((n, 1, LANES), jnp.int32),
                pltpu.SMEM((n, 1, LANES), jnp.int32),
                pltpu.SemaphoreType.DMA((groups,)),
            ],
            compiler_params=pltpu.CompilerParams(collective_id=0, has_side_effects=True),
            name="propensity",
        )(
            query,
            context_features,
            candidates,
            scalars,
            item_table,
            w_first,
            w_second,
            w_score,
        )
        return section, weight.reshape(-1)

    split = P(("dp", "item"))
    rows = P(("dp", "item"), None)
    return jax.shard_map(
        body,
        mesh=mesh,
        in_specs=(rows, rows, rows, rows, split, split, split, P(), P(), P()),
        out_specs=(rows, split),
        check_vma=False,
    )
```

profile of v0, /device:TPU:0, one launch (start us, length us, event | category | flops | bytes accessed | tf_op | source)
XLA Modules:
  0.0 26.6 jit_solution(17484200339713376313)
XLA Ops:
  2.6 0.5 %compare_select_fusion.1.scalar_hbm = s32[1,128]{1,0:T(1,128)} fusion(s32[]{:T(128)} %bitcast.6, s32[]{:T(128)} %bitcast.5, s32[]{:T(128)} %bitcast.4), kind=kLoop, calls=%fused_computation.1 | loop fusion | flops 512 | bytes 524 | tf_op jit(solution)/shard_map/jit(_where)/select_n | solution.py:368
  3.1 21.7 %propensity.1 = (f32[1,1024]{1,0:T(1,128)S(1)}, f32[1,1]{1,0:T(1,128)S(1)}) custom-call(bf16[1,256]{1,0:T(2,128)(2,1)} %query_hbm.1, bf16[1,512]{1,0:T(2,128)(2,1)} %feature_hbm.1, s32[1,1024]{1,0:T(1,128)} %cand_hbm.1, s32[1,128]{1,0:T(1,128)} %compare_select_fusion.1.scalar_hbm, bf16[2048,256]{1,0:T(8,128)(2,1)} %table_hbm.1, bf16[768,512]{1,0:T(8,128)(2,1)} %first_hbm.1, ...), custom_call_target="tpu_custom_call" | custom-call | tf_op jit(solution)/shard_map/propensity/pallas_call | solution.py:369
  24.9 0.6 %copy.14 = f32[1,1024]{1,0:T(1,128)} copy(f32[1,1024]{1,0:T(1,128)S(1)} %get-tuple-element.6) | data formatting | bytes 8192
where the time goes:
time: 26.8 us; the launch traced here: 26.6 us
  Pallas kernels  21.7 us (81%)
  between operations  3.74 us (14%)
  local copies, waits for them, and re-layouts  0.6 us (2%)
  other arithmetic  0.54 us (2%)
    pallas_call x1, Pallas kernels, body(): pl.pallas_call(functools.partial(kernel, dp_size, item_size, groups, cap)...  21.7 us
    unnamed x1, local copies, waits for them, and re-layouts  0.6 us
    select_n x1, other arithmetic, body(): jnp.where(lane == 0, lengths, jnp.where(lane == 1, logged_slot, logging_p...  0.54 us

commit v1 on v0

--- a/solution.py
+++ b/solution.py
@@ -37,7 +37,9 @@
     query_hbm,
     feature_hbm,
     cand_hbm,
-    scalar_hbm,
+    length_hbm,
+    slot_hbm,
+    prop_hbm,
     table_hbm,
     first_hbm,
     second_hbm,
@@ -47,7 +49,9 @@
     query_ref,
     feature_ref,
     cand_ref,
-    scalar_ref,
+    length_ref,
+    slot_ref,
+    prop_ref,
     score_ref,
     table,
     first,
@@ -113,7 +117,9 @@
                 (table_hbm, table),
                 (second_hbm, second_w),
                 (score_hbm, score_ref),
-                (scalar_hbm, scalar_ref),
+                (length_hbm, length_ref),
+                (slot_hbm, slot_ref),
+                (prop_hbm, prop_ref),
             ]
         )
     ]
@@ -209,6 +215,7 @@
     score_rows = jnp.broadcast_to(score_ref[...].reshape(1, hidden_width), (LANES, hidden_width))
     hidden_tiles = hidden_width // LANES
     tall = items.shape[1]
+    flat = items.reshape(item_rows * tall, LANES)
     step = math.gcd(256, item_rows)
 
     @pl.loop(0, item_rows // step)
@@ -216,11 +223,15 @@
         part = pl.ds(pl.multiple_of(i * step, step), step)
         block = table[part]
         projected = dot(block, first[feature_width:, :], NN)
+        base = pl.multiple_of(i * (step * tall), step * tall)
+
+        def put(j, value):
+            flat[pl.ds(base + j, step, stride=tall), :] = value
+
         for j in range(hidden_tiles):
-            items[part, j] = projected[:, j * LANES : (j + 1) * LANES]
+            put(j, projected[:, j * LANES : (j + 1) * LANES])
         for j in range(width // LANES):
-            items[part, hidden_tiles + j] = block[:, j * LANES : (j + 1) * LANES].astype(F32)
-
+            put(hidden_tiles + j, block[:, j * LANES : (j + 1) * LANES].astype(F32))
 
     def to_scalar(group):
         rows_here = pl.ds(group * members, members)
@@ -235,7 +246,7 @@
         to_scalar(group).wait()
         for r in range(cap):
             for c in range(members):
-                at = jnp.clip(wanted_at[group * members + c, 0, r], 0, item_rows - 1)
+                at = wanted_at[group * members + c, 0, r]
                 place = (group * cap + r) * members + c
                 found[pl.ds(place * tall, tall)] = items[at]
         count = cap * members
@@ -258,48 +269,31 @@
             result = jnp.where(lane == gen_at + r, gen, result)
         return result
 
-    def normalizers():
-        logits = dot(recv1[:, 0, :width].astype(BF16), table[...], NT)
+    def normalizers(group):
+        rows_here = pl.ds(group * members, members)
+        logits = dot(recv1[rows_here, 0, :width].astype(BF16), table[...], NT)
         local_max = jnp.max(logits, axis=1, keepdims=True)
         local_sum = jnp.sum(jnp.exp(logits - local_max), axis=1, keepdims=True)
         return local_max, local_sum
 
     order = sorted(range(groups), key=lambda g: min(g, groups - g))
-    order = order[:-2] + order[:-3:-1]
-    results = {}
-    waited = set()
-
-    def wait_group(group):
-        if group not in waited:
-            waited.add(group)
-            wait_rows(recv1, members - 1 if group == 0 else members, arrive_sem.at[group])
-            rows_here = pl.ds(group * members, members)
-            wanted_v[rows_here] = recv1[rows_here, :, width + hidden_width :].astype(jnp.int32)
-            to_scalar(group).start()
-
-    for group in order[:-2]:
-        wait_group(group)
-        results[group] = rank_group(group)
-    for group in order[-2:]:
-        wait_group(group)
-    local_max, local_sum = normalizers()
-
-    def finish(group):
-        mine = slice(group * members, (group + 1) * members)
-        result = jnp.where(lane == max_at, local_max[mine], results[group])
-        result = jnp.where(lane == max_at + 1, local_sum[mine], result)
-        send2[pl.ds(group * members, members), 0, :] = result
+    for group in order:
+        rows_here = pl.ds(group * members, members)
+        wait_rows(recv1, members - 1 if group == 0 else members, arrive_sem.at[group])
+        asked_here = recv1[rows_here, :, width + hidden_width :].astype(jnp.int32)
+        wanted_v[rows_here] = jnp.clip(asked_here, 0, item_rows - 1)
+        to_scalar(group).start()
+        local_max, local_sum = normalizers(group)
+        result = rank_group(group)
+        result = jnp.where(lane == max_at, local_max, result)
+        result = jnp.where(lane == max_at + 1, local_sum, result)
+        send2[rows_here, 0, :] = result
         give_back(group)
-
-    for group in reversed(order[:-2]):
-        finish(group)
-    own_back = pltpu.make_async_copy(
-        send2.at[pl.ds(member_me, 1)], recv2.at[pl.ds(me, 1)], own_sem.at[1]
-    )
-    own_back.start()
-    for group in order[-2:]:
-        results[group] = rank_group(group)
-        finish(group)
+        if group == 0:
+            own_back = pltpu.make_async_copy(
+                send2.at[pl.ds(member_me, 1)], recv2.at[pl.ds(me, 1)], own_sem.at[1]
+            )
+            own_back.start()
     own_back.wait()
     wait_rows(send1, n - 1, send_sem.at[0])
     wait_rows(recv2, n - 1, return_sem)
@@ -322,7 +316,7 @@
     peak = jnp.max(maxima, axis=0, keepdims=True)
     log_norm = peak + jnp.log(jnp.sum(sums * jnp.exp(maxima - peak), axis=0, keepdims=True))
 
-    length = scalar_ref[:, 0:1]
+    length = length_ref[0]
     position = lax.broadcasted_iota(jnp.int32, (1, slots), 1)
     live = position < length
     masked = jnp.where(live, score, -1e30)
@@ -333,10 +327,11 @@
     section = jnp.where(
         live, score - rank_norm + gen - log_norm + math.log(item_rows * n), 0.0
     )
-    chosen = jnp.sum(jnp.where(position == scalar_ref[:, 1:2], section, 0.0), axis=1, keepdims=True)
-    prop = scalar_ref[:, 2:3].astype(F32) / 1024.0
+    chosen = jnp.sum(jnp.where(position == slot_ref[0], section, 0.0), axis=1, keepdims=True)
+    count = jnp.full((1, 1), length, jnp.int32).astype(F32)
+    prop = jnp.full((1, 1), prop_ref[0], jnp.int32).astype(F32) / 1024.0
     section_ref[...] = section
-    weight_ref[...] = chosen + jnp.log(length.astype(F32)) - jnp.log(prop)
+    weight_ref[...] = chosen + jnp.log(count) - jnp.log(prop)
     wait_rows(send2, n - 1, send_sem.at[1])
 
 
@@ -364,21 +359,21 @@
         tall = round_up((width + hidden_width) // LANES, 8)
         vmem = pl.BlockSpec(memory_space=pltpu.VMEM)
         groups = math.gcd(4, item_size)
-        lane = lax.broadcasted_iota(jnp.int32, (1, LANES), 1)
-        scalars = jnp.where(lane == 0, lengths, jnp.where(lane == 1, logged_slot, logging_prop))
         section, weight = pl.pallas_call(
             functools.partial(kernel, dp_size, item_size, groups, cap),
             out_shape=(
                 pltpu.VMEM((1, slots), F32),
                 pltpu.VMEM((1, 1), F32),
             ),
-            in_specs=[pl.BlockSpec(memory_space=pltpu.HBM)] * 8,
+            in_specs=[pl.BlockSpec(memory_space=pltpu.HBM)] * 10,
             out_specs=(vmem, vmem),
             scratch_shapes=[
                 pltpu.VMEM(query.shape, BF16),
                 pltpu.VMEM(context_features.shape, BF16),
                 pltpu.VMEM(candidates.shape, jnp.int32),
-                pltpu.VMEM((1, LANES), jnp.int32),
+                pltpu.SMEM((1,), jnp.int32),
+                pltpu.SMEM((1,), jnp.int32),
+                pltpu.SMEM((1,), jnp.int32),
                 pltpu.VMEM(w_score.shape, BF16),
                 pltpu.VMEM(item_table.shape, BF16),
                 pltpu.VMEM(w_first.shape, BF16),
@@ -387,7 +382,7 @@
                 pltpu.VMEM((n, 1, message), F32),
                 pltpu.VMEM((n, 1, LANES), F32),
                 pltpu.VMEM((n, 1, LANES), F32),
-                pltpu.SemaphoreType.DMA((8,)),
+                pltpu.SemaphoreType.DMA((10,)),
                 pltpu.SemaphoreType.DMA((2,)),
                 pltpu.SemaphoreType.DMA((groups,)),
                 pltpu.SemaphoreType.DMA,
@@ -404,7 +399,9 @@
             query,
             context_features,
             candidates,
-            scalars,
+            lengths,
+            logged_slot,
+            logging_prop,
             item_table,
             w_first,
             w_second,

time: 26.8 us -> 27.8 us (1.037)
  Pallas kernels: 21.7 us -> 23.2 us
  other arithmetic: 0.54 us -> 0 us
    pallas_call x1, Pallas kernels: 21.7 us -> 23.2 us  [body(): pl.pallas_call(functools.partial(kernel, dp_size, item_size, groups, cap)...]
    select_n x1 -> x0, other arithmetic: 0.54 us -> none  [body(): jnp.where(lane == 0, lengths, jnp.where(lane == 1, logged_slot, logging_p...]
where the time goes in v1:
time: 27.8 us; the launch traced here: 27.6 us
  Pallas kernels  23.2 us (83%)
  between operations  3.74 us (13%)
  local copies, waits for them, and re-layouts  0.6 us (2%)
    pallas_call x1, Pallas kernels, body(): pl.pallas_call(functools.partial(kernel, dp_size, item_size, groups, cap)...  23.2 us
    unnamed x1, local copies, waits for them, and re-layouts  0.6 us

profile of v1, /device:TPU:0, one launch (start us, length us, event | category | flops | bytes accessed | tf_op | source)
XLA Modules:
  0.0 27.6 jit_solution(13785277338853201730)
XLA Ops:
  2.6 23.2 %propensity.1 = (f32[1,1024]{1,0:T(1,128)S(1)}, f32[1,1]{1,0:T(1,128)S(1)}) custom-call(bf16[1,256]{1,0:T(2,128)(2,1)} %query_hbm.1, bf16[1,512]{1,0:T(2,128)(2,1)} %feature_hbm.1, s32[1,1024]{1,0:T(1,128)} %cand_hbm.1, s32[1]{0:T(128)S(6)} %copy.16.length_hbm, s32[1]{0:T(128)S(6)} %copy.17.slot_hbm, s32[1]{0:T(128)S(6)} %copy.18.prop_hbm, ...), custom_call_target="tpu_custom_call" | custom-call | tf_op jit(solution)/shard_map/propensity/pallas_call | solution.py:362
  25.9 0.6 %copy.14 = f32[1,1024]{1,0:T(1,128)} copy(f32[1,1024]{1,0:T(1,128)S(1)} %get-tuple-element.6) | data formatting | bytes 8192

commit v2 on v1

--- a/solution.py
+++ b/solution.py
@@ -56,6 +56,7 @@
     table,
     first,
     second_w,
+    send_ids,
     send1,
     recv1,
     send2,
@@ -63,13 +64,12 @@
     load_sem,
     send_sem,
     arrive_sem,
+    index_sem,
     return_sem,
     own_sem,
     items,
     found,
-    wanted_v,
-    wanted_at,
-    index_sem,
+    wanted,
 ):
     n = dp_size * item_size
     item_rows, width = table.shape
@@ -158,24 +158,61 @@
     ).astype(F32)
     parts = jnp.concatenate([held * high, held * low], axis=0).astype(BF16)
     asked = dot(parts, at_rank.astype(BF16), NT)
-    asked = asked[:n] * float(LANES) + asked[n:]
+    asked = (asked[:n] * float(LANES) + asked[n:]).astype(jnp.int32)
+    tall = items.shape[1]
+    scale = tall
+    send_ids[:, 0, :] = jnp.clip(asked, 0, item_rows - 1) * scale
 
     for load in loads[1:4]:
         load.wait()
-    context_part = dot(feature_ref[...], first[:feature_width, :], NN)
-    send1[:, 0, :width] = jnp.broadcast_to(query_ref[...].astype(F32), (n, width))
-    send1[:, 0, width : width + hidden_width] = jnp.broadcast_to(context_part, (n, hidden_width))
-    send1[:, 0, width + hidden_width :] = asked
-
+    context_part = dot(feature_ref[...], first[:feature_width, :], NN) * 0.5
+    send1[0, :, :width] = query_ref[...].astype(F32)
+    send1[0, :, width:] = context_part
+    for load in loads[4:]:
+        load.wait()
+    second_w[...] = second_w[...] * jnp.asarray(0.5, BF16)
+
+    flat = items.reshape(item_rows * tall, LANES)
+    hidden_tiles = hidden_width // LANES
+    step = math.gcd(256, item_rows)
+    strips = item_rows // step
+    early = strips * 4 // 8
+
+    def project(start, stop):
+        @pl.loop(start, stop)
+        def visit(i):
+            part = pl.ds(pl.multiple_of(i * step, step), step)
+            block = table[part]
+            projected = dot(block, first[feature_width:, :], NN) * 0.5
+            base = pl.multiple_of(i * (step * tall), step * tall)
+
+            def put(j, value):
+                flat[pl.ds(base + j, step, stride=tall), :] = value
+
+            for j in range(hidden_tiles):
+                put(j, projected[:, j * LANES : (j + 1) * LANES])
+            for j in range(width // LANES):
+                put(hidden_tiles + j, block[:, j * LANES : (j + 1) * LANES].astype(F32))
+
+    project(0, early)
     pl.semaphore_wait(barrier, n - 1)
 
     def ask(offset):
         seen = (groups - offset) % groups
 
         def act(member, peer, where):
+            slot = pl.ds(seen * members + member_me, 1)
             pltpu.make_async_remote_copy(
-                src_ref=send1.at[pl.ds(peer, 1)],
-                dst_ref=recv1.at[pl.ds(seen * members + member_me, 1)],
+                src_ref=send_ids.at[pl.ds(peer, 1)],
+                dst_ref=wanted.at[slot],
+                send_sem=send_sem.at[2],
+                recv_sem=index_sem.at[seen],
+                device_id=where,
+                device_id_type=pl.DeviceIdType.MESH,
+            ).start()
+            pltpu.make_async_remote_copy(
+                src_ref=send1,
+                dst_ref=recv1.at[slot],
                 send_sem=send_sem.at[0],
                 recv_sem=arrive_sem.at[seen],
                 device_id=where,
@@ -184,118 +221,119 @@
 
         each_peer(offset, act)
 
-    def give_back(offset):
-        def act(member, peer, where):
-            pltpu.make_async_remote_copy(
-                src_ref=send2.at[pl.ds(offset * members + member, 1)],
-                dst_ref=recv2.at[pl.ds(me, 1)],
-                send_sem=send_sem.at[1],
-                recv_sem=return_sem,
-                device_id=where,
-                device_id_type=pl.DeviceIdType.MESH,
-            ).start()
-
-        each_peer(offset, act)
+    def give_back(group):
+        offset = group
+
+        @pl.loop(0, members)
+        def visit(j):
+            member = lax.rem(member_me + j, members)
+            peer, where = device(offset, member)
+
+            @pl.when(peer != me)
+            def send():
+                pltpu.make_async_remote_copy(
+                    src_ref=send2.at[pl.ds(offset * members + member, 1)],
+                    dst_ref=recv2.at[pl.ds(me, 1)],
+                    send_sem=send_sem.at[1],
+                    recv_sem=return_sem,
+                    device_id=where,
+                    device_id_type=pl.DeviceIdType.MESH,
+                ).start()
+
+    def wait_ids(group, expected):
+        rows = wanted.at[pl.ds(group * members, expected)]
+        pltpu.make_async_copy(
+            send_ids.at[pl.ds(0, expected)], rows, index_sem.at[group]
+        ).wait()
 
     def wait_rows(buffer, count, semaphore):
         rows = buffer.at[pl.ds(0, count)]
         pltpu.make_async_copy(rows, rows, semaphore).wait()
 
-    own_ask = pltpu.make_async_copy(
-        send1.at[pl.ds(me, 1)], recv1.at[pl.ds(member_me, 1)], own_sem.at[0]
-    )
-    own_ask.start()
     for offset in far_first:
         ask(offset)
-    for load in loads[4:]:
-        load.wait()
+    own_ids = pltpu.make_async_copy(
+        send_ids.at[pl.ds(me, 1)], wanted.at[pl.ds(member_me, 1)], own_sem.at[0]
+    )
+    own_ids.start()
+    own_ask = pltpu.make_async_copy(send1, recv1.at[pl.ds(member_me, 1)], own_sem.at[1])
+    own_ask.start()
+    project(early, strips)
+    own_ids.wait()
     own_ask.wait()
 
     lane = lax.broadcasted_iota(jnp.int32, (members, LANES), 1)
+    row = lax.broadcasted_iota(jnp.int32, (members, LANES), 0)
     score_rows = jnp.broadcast_to(score_ref[...].reshape(1, hidden_width), (LANES, hidden_width))
-    hidden_tiles = hidden_width // LANES
-    tall = items.shape[1]
-    flat = items.reshape(item_rows * tall, LANES)
-    step = math.gcd(256, item_rows)
-
-    @pl.loop(0, item_rows // step)
-    def project(i):
-        part = pl.ds(pl.multiple_of(i * step, step), step)
-        block = table[part]
-        projected = dot(block, first[feature_width:, :], NN)
-        base = pl.multiple_of(i * (step * tall), step * tall)
-
-        def put(j, value):
-            flat[pl.ds(base + j, step, stride=tall), :] = value
-
-        for j in range(hidden_tiles):
-            put(j, projected[:, j * LANES : (j + 1) * LANES])
-        for j in range(width // LANES):
-            put(hidden_tiles + j, block[:, j * LANES : (j + 1) * LANES].astype(F32))
-
-    def to_scalar(group):
-        rows_here = pl.ds(group * members, members)
-        return pltpu.make_async_copy(
-            wanted_v.at[rows_here], wanted_at.at[rows_here], index_sem.at[group]
-        )
-
-    def rank_group(group):
+    count = cap * members
+    copies = LANES // members
+    split = math.gcd(4, copies)
+    part_rows = item_rows // split
+
+    def rank_group(turn, group):
         rows_here = pl.ds(group * members, members)
         query = recv1[rows_here, 0, :width]
-        context = recv1[rows_here, 0, width : width + hidden_width]
-        to_scalar(group).wait()
+        context = recv1[rows_here, 0, width:]
+        blank = jnp.zeros_like(query)
+        logits = None
+        for part in range(split):
+            spread = jnp.concatenate(
+                [query if j % split == part else blank for j in range(copies)], axis=0
+            ).astype(BF16)
+            partial = dot(table[part * part_rows : (part + 1) * part_rows], spread, NT)
+            logits = partial if logits is None else logits + partial
+        top = jnp.max(logits, axis=0, keepdims=True)
+        turns = [members << k for k in range(split.bit_length() - 1)]
+        for shift in turns:
+            top = jnp.maximum(top, pltpu.roll(top, shift, 1))
+        mass = jnp.sum(jnp.exp(logits - top), axis=0, keepdims=True)
+        for shift in turns:
+            mass = mass + pltpu.roll(mass, shift, 1)
+
+        def own_lane(value):
+            return jnp.sum(jnp.where(lane == row, value, 0.0), axis=1, keepdims=True)
+
         for r in range(cap):
             for c in range(members):
-                at = wanted_at[group * members + c, 0, r]
-                place = (group * cap + r) * members + c
-                found[pl.ds(place * tall, tall)] = items[at]
-        count = cap * members
+                at = wanted[group * members + c, 0, r]
+                place = (turn * cap + r) * members + c
+                found[pl.ds(place * tall, tall)] = flat[pl.ds(at, tall)]
 
         def found_tile(j):
-            return found[pl.ds(group * count * tall + j, count, stride=tall), :]
+            return found[pl.ds(turn * count * tall + j, count, stride=tall), :]
 
         item_part = jnp.concatenate([found_tile(j) for j in range(hidden_tiles)], axis=1)
         rows = jnp.concatenate(
             [found_tile(hidden_tiles + j) for j in range(width // LANES)], axis=1
         )
-        hidden = silu(item_part + jnp.concatenate([context] * cap, axis=0)).astype(BF16)
-        second = silu(dot(hidden, second_w[...], NN)).astype(BF16)
+        half = item_part + jnp.concatenate([context] * cap, axis=0)
+        hidden = (half + half * jnp.tanh(half)).astype(BF16)
+        half = dot(hidden, second_w[...], NN)
+        second = (half + half * jnp.tanh(half)).astype(BF16)
         score = dot(second, score_rows, NT)
-        result = jnp.zeros((members, LANES), F32)
+        result = jnp.where(lane == max_at, own_lane(top), own_lane(mass))
         for r in range(cap):
             mine = slice(r * members, (r + 1) * members)
             gen = jnp.sum(rows[mine] * query, axis=1, keepdims=True)
             result = jnp.where(lane == r, score[mine], result)
             result = jnp.where(lane == gen_at + r, gen, result)
-        return result
-
-    def normalizers(group):
-        rows_here = pl.ds(group * members, members)
-        logits = dot(recv1[rows_here, 0, :width].astype(BF16), table[...], NT)
-        local_max = jnp.max(logits, axis=1, keepdims=True)
-        local_sum = jnp.sum(jnp.exp(logits - local_max), axis=1, keepdims=True)
-        return local_max, local_sum
-
-    order = sorted(range(groups), key=lambda g: min(g, groups - g))
-    for group in order:
-        rows_here = pl.ds(group * members, members)
-        wait_rows(recv1, members - 1 if group == 0 else members, arrive_sem.at[group])
-        asked_here = recv1[rows_here, :, width + hidden_width :].astype(jnp.int32)
-        wanted_v[rows_here] = jnp.clip(asked_here, 0, item_rows - 1)
-        to_scalar(group).start()
-        local_max, local_sum = normalizers(group)
-        result = rank_group(group)
-        result = jnp.where(lane == max_at, local_max, result)
-        result = jnp.where(lane == max_at + 1, local_sum, result)
         send2[rows_here, 0, :] = result
+
+    near_first = sorted(range(groups), key=lambda g: min(g, groups - g))
+    order = near_first
+    for turn, group in enumerate(order):
+        expected = members - 1 if group == 0 else members
+        wait_ids(group, expected)
+        wait_rows(recv1, expected, arrive_sem.at[group])
+        rank_group(turn, group)
         give_back(group)
-        if group == 0:
-            own_back = pltpu.make_async_copy(
-                send2.at[pl.ds(member_me, 1)], recv2.at[pl.ds(me, 1)], own_sem.at[1]
-            )
-            own_back.start()
+    own_back = pltpu.make_async_copy(
+        send2.at[pl.ds(member_me, 1)], recv2.at[pl.ds(me, 1)], own_sem.at[2]
+    )
+    own_back.start()
     own_back.wait()
-    wait_rows(send1, n - 1, send_sem.at[0])
+    wait_rows(send_ids, n - 1, send_sem.at[2])
+    wait_rows(recv1, n - 1, send_sem.at[0])
     wait_rows(recv2, n - 1, return_sem)
 
     back = recv2[:, 0, :]
@@ -355,7 +393,7 @@
         cap = max(2, 3 * slots // (2 * n))
         width = query.shape[1]
         hidden_width = w_first.shape[1]
-        message = width + hidden_width + LANES
+        message = width + hidden_width
         tall = round_up((width + hidden_width) // LANES, 8)
         vmem = pl.BlockSpec(memory_space=pltpu.VMEM)
         groups = math.gcd(4, item_size)
@@ -378,20 +416,20 @@
                 pltpu.VMEM(item_table.shape, BF16),
                 pltpu.VMEM(w_first.shape, BF16),
                 pltpu.VMEM(w_second.shape, BF16),
-                pltpu.VMEM((n, 1, message), F32),
+                pltpu.VMEM((n, 1, LANES), jnp.int32),
+                pltpu.VMEM((1, 1, message), F32),
                 pltpu.VMEM((n, 1, message), F32),
                 pltpu.VMEM((n, 1, LANES), F32),
                 pltpu.VMEM((n, 1, LANES), F32),
                 pltpu.SemaphoreType.DMA((10,)),
-                pltpu.SemaphoreType.DMA((2,)),
+                pltpu.SemaphoreType.DMA((3,)),
+                pltpu.SemaphoreType.DMA((groups,)),
                 pltpu.SemaphoreType.DMA((groups,)),
                 pltpu.SemaphoreType.DMA,
-                pltpu.SemaphoreType.DMA((2,)),
+                pltpu.SemaphoreType.DMA((3,)),
                 pltpu.VMEM((item_table.shape[0], tall, LANES), F32),
                 pltpu.VMEM((n * cap * tall + tall, LANES), F32),
-                pltpu.VMEM((n, 1, LANES), jnp.int32),
                 pltpu.SMEM((n, 1, LANES), jnp.int32),
-                pltpu.SemaphoreType.DMA((groups,)),
             ],
             compiler_params=pltpu.CompilerParams(collective_id=0, has_side_effects=True),
             name="propensity",

time: 27.8 us -> 25.5 us (0.917)
  Pallas kernels: 23.2 us -> 21 us
    pallas_call x1, Pallas kernels: 23.2 us -> 21 us  [body(): pl.pallas_call(functools.partial(kernel, dp_size, item_size, groups, cap)...]
where the time goes in v2:
time: 25.5 us; the launch traced here: 25.3 us
  Pallas kernels  21 us (82%)
  between operations  3.74 us (15%)
  local copies, waits for them, and re-layouts  0.6 us (2%)
    pallas_call x1, Pallas kernels, body(): pl.pallas_call(functools.partial(kernel, dp_size, item_size, groups, cap)...  21 us
    unnamed x1, local copies, waits for them, and re-layouts  0.6 us

profile of v2, /device:TPU:0, one launch (start us, length us, event | category | flops | bytes accessed | tf_op | source)
XLA Modules:
  0.0 25.3 jit_solution(9681206745427714106)
XLA Ops:
  2.6 21.0 %propensity.1 = (f32[1,1024]{1,0:T(1,128)S(1)}, f32[1,1]{1,0:T(1,128)S(1)}) custom-call(bf16[1,256]{1,0:T(2,128)(2,1)} %query_hbm.1, bf16[1,512]{1,0:T(2,128)(2,1)} %feature_hbm.1, s32[1,1024]{1,0:T(1,128)} %cand_hbm.1, s32[1]{0:T(128)S(6)} %copy.16.length_hbm, s32[1]{0:T(128)S(6)} %copy.17.slot_hbm, s32[1]{0:T(128)S(6)} %copy.18.prop_hbm, ...), custom_call_target="tpu_custom_call" | custom-call | tf_op jit(solution)/shard_map/propensity/pallas_call | solution.py:400
  23.6 0.6 %copy.14 = f32[1,1024]{1,0:T(1,128)} copy(f32[1,1024]{1,0:T(1,128)S(1)} %get-tuple-element.6) | data formatting | bytes 8192

commit v3 on v2

--- a/solution.py
+++ b/solution.py
@@ -91,7 +91,7 @@
         return dp * item_size + item, {"dp": dp, "item": item}
 
     def each_peer(offset, act):
-        @pl.loop(1 if offset == 0 else 0, members)
+        @pl.loop(1 if isinstance(offset, int) else 0, members)
         def visit(j):
             member = lax.rem(member_me + j, members)
             peer, where = device(offset, member)
@@ -102,7 +102,10 @@
     def greet(member, peer, where):
         pl.semaphore_signal(barrier, inc=1, device_id=where, device_id_type=pl.DeviceIdType.MESH)
 
-    far_first = sorted(range(groups), key=lambda g: -min(g, groups - g))
+    end = jnp.where(2 * run_me < groups, groups - 1, 0)
+    far = lax.rem(end - run_me + groups, groups)
+    middle = [jnp.where(far <= k, k + 1, k) for k in range(1, groups - 1)]
+    far_first = ([far] if groups > 1 else []) + middle[::-1] + [0]
     for offset in far_first:
         each_peer(offset, greet)
 
@@ -159,7 +162,8 @@
     parts = jnp.concatenate([held * high, held * low], axis=0).astype(BF16)
     asked = dot(parts, at_rank.astype(BF16), NT)
     asked = (asked[:n] * float(LANES) + asked[n:]).astype(jnp.int32)
-    tall = items.shape[1]
+    tall = items.shape[0] // item_rows
+    lines = tall - 1
     scale = tall
     send_ids[:, 0, :] = jnp.clip(asked, 0, item_rows - 1) * scale
 
@@ -172,11 +176,10 @@
         load.wait()
     second_w[...] = second_w[...] * jnp.asarray(0.5, BF16)
 
-    flat = items.reshape(item_rows * tall, LANES)
     hidden_tiles = hidden_width // LANES
     step = math.gcd(256, item_rows)
     strips = item_rows // step
-    early = strips * 4 // 8
+    early = lax.div(strips * jnp.maximum(groups - 2 * run_me, 0), groups)
 
     def project(start, stop):
         @pl.loop(start, stop)
@@ -187,7 +190,7 @@
             base = pl.multiple_of(i * (step * tall), step * tall)
 
             def put(j, value):
-                flat[pl.ds(base + j, step, stride=tall), :] = value
+                items[pl.ds(base + j, step, stride=tall), :] = value
 
             for j in range(hidden_tiles):
                 put(j, projected[:, j * LANES : (j + 1) * LANES])
@@ -198,7 +201,7 @@
     pl.semaphore_wait(barrier, n - 1)
 
     def ask(offset):
-        seen = (groups - offset) % groups
+        seen = lax.rem(groups - offset, groups)
 
         def act(member, peer, where):
             slot = pl.ds(seen * members + member_me, 1)
@@ -250,7 +253,7 @@
         rows = buffer.at[pl.ds(0, count)]
         pltpu.make_async_copy(rows, rows, semaphore).wait()
 
-    for offset in far_first:
+    for offset in (far_first[:1] + far_first[:0:-1]):
         ask(offset)
     own_ids = pltpu.make_async_copy(
         send_ids.at[pl.ds(me, 1)], wanted.at[pl.ds(member_me, 1)], own_sem.at[0]
@@ -263,17 +266,55 @@
     own_ask.wait()
 
     lane = lax.broadcasted_iota(jnp.int32, (members, LANES), 1)
-    row = lax.broadcasted_iota(jnp.int32, (members, LANES), 0)
-    score_rows = jnp.broadcast_to(score_ref[...].reshape(1, hidden_width), (LANES, hidden_width))
-    count = cap * members
-    copies = LANES // members
-    split = math.gcd(4, copies)
+    score_row = score_ref[...].reshape(1, hidden_width).astype(F32)
+    copies = max(1, LANES // n)
+    split = 1 << (math.gcd(4, copies).bit_length() - 1)
     part_rows = item_rows // split
 
-    def rank_group(turn, group):
-        rows_here = pl.ds(group * members, members)
-        query = recv1[rows_here, 0, :width]
-        context = recv1[rows_here, 0, width:]
+    def rank_groups(turn, batch):
+        count = cap * members * len(batch)
+        base = turn * cap * members
+        for r in range(cap):
+            for b, group in enumerate(batch):
+                for c in range(members):
+                    at = wanted[group * members + c, 0, r]
+                    place = base + (r * len(batch) + b) * members + c
+                    found[pl.ds(place * tall, lines)] = items[pl.ds(at, lines)]
+
+        def found_tile(j):
+            return found[pl.ds(base * tall + j, count, stride=tall), :]
+
+        def stacked_rows(low, high):
+            return jnp.concatenate(
+                [recv1[pl.ds(group * members, members), 0, low:high] for group in batch], axis=0
+            )
+
+        query = stacked_rows(0, width)
+        context = stacked_rows(width, width + hidden_width)
+        item_part = jnp.concatenate([found_tile(j) for j in range(hidden_tiles)], axis=1)
+        rows = jnp.concatenate(
+            [found_tile(hidden_tiles + j) for j in range(width // LANES)], axis=1
+        )
+        half = item_part + jnp.concatenate([context] * cap, axis=0)
+        hidden = (half + half * jnp.tanh(half)).astype(BF16)
+        half = dot(hidden, second_w[...], NN)
+        second = (half + half * jnp.tanh(half)).astype(BF16).astype(F32) * score_row
+        deep = len(batch) * members
+        lanes = lax.broadcasted_iota(jnp.int32, (deep, LANES), 1)
+        result = jnp.zeros((deep, LANES), F32)
+        for r in range(cap):
+            mine = slice(r * deep, (r + 1) * deep)
+            score = jnp.sum(second[mine], axis=1, keepdims=True)
+            gen = jnp.sum(rows[mine] * query, axis=1, keepdims=True)
+            result = jnp.where(lanes == r, score, result)
+            result = jnp.where(lanes == gen_at + r, gen, result)
+        for b, group in enumerate(batch):
+            send2[pl.ds(group * members, members), 0, :] = result[
+                b * members : (b + 1) * members
+            ]
+
+    def normalizers():
+        query = recv1[:, 0, :width]
         blank = jnp.zeros_like(query)
         logits = None
         for part in range(split):
@@ -283,50 +324,48 @@
             partial = dot(table[part * part_rows : (part + 1) * part_rows], spread, NT)
             logits = partial if logits is None else logits + partial
         top = jnp.max(logits, axis=0, keepdims=True)
-        turns = [members << k for k in range(split.bit_length() - 1)]
-        for shift in turns:
-            top = jnp.maximum(top, pltpu.roll(top, shift, 1))
         mass = jnp.sum(jnp.exp(logits - top), axis=0, keepdims=True)
-        for shift in turns:
+        peak = top
+        shifts = [n << k for k in range(split.bit_length() - 1)]
+        for shift in shifts:
+            peak = jnp.maximum(peak, pltpu.roll(peak, shift, 1))
+        mass = mass * jnp.exp(top - peak)
+        for shift in shifts:
             mass = mass + pltpu.roll(mass, shift, 1)
+        return peak, mass
+
+    def finish(group, peak, mass):
+        rows_here = pl.ds(group * members, members)
+        across = (members, peak.shape[1])
+        mine = lax.broadcasted_iota(jnp.int32, across, 1) == group * members + (
+            lax.broadcasted_iota(jnp.int32, across, 0)
+        )
 
         def own_lane(value):
-            return jnp.sum(jnp.where(lane == row, value, 0.0), axis=1, keepdims=True)
-
-        for r in range(cap):
-            for c in range(members):
-                at = wanted[group * members + c, 0, r]
-                place = (turn * cap + r) * members + c
-                found[pl.ds(place * tall, tall)] = flat[pl.ds(at, tall)]
-
-        def found_tile(j):
-            return found[pl.ds(turn * count * tall + j, count, stride=tall), :]
-
-        item_part = jnp.concatenate([found_tile(j) for j in range(hidden_tiles)], axis=1)
-        rows = jnp.concatenate(
-            [found_tile(hidden_tiles + j) for j in range(width // LANES)], axis=1
-        )
-        half = item_part + jnp.concatenate([context] * cap, axis=0)
-        hidden = (half + half * jnp.tanh(half)).astype(BF16)
-        half = dot(hidden, second_w[...], NN)
-        second = (half + half * jnp.tanh(half)).astype(BF16)
-        score = dot(second, score_rows, NT)
-        result = jnp.where(lane == max_at, own_lane(top), own_lane(mass))
-        for r in range(cap):
-            mine = slice(r * members, (r + 1) * members)
-            gen = jnp.sum(rows[mine] * query, axis=1, keepdims=True)
-            result = jnp.where(lane == r, score[mine], result)
-            result = jnp.where(lane == gen_at + r, gen, result)
-        send2[rows_here, 0, :] = result
-
-    near_first = sorted(range(groups), key=lambda g: min(g, groups - g))
-    order = near_first
-    for turn, group in enumerate(order):
-        expected = members - 1 if group == 0 else members
-        wait_ids(group, expected)
-        wait_rows(recv1, expected, arrive_sem.at[group])
-        rank_group(turn, group)
-        give_back(group)
+            return jnp.sum(jnp.where(mine, value, 0.0), axis=1, keepdims=True)
+
+        result = jnp.where(lane == max_at, own_lane(peak), send2[rows_here, 0, :])
+        send2[rows_here, 0, :] = jnp.where(lane == max_at + 1, own_lane(mass), result)
+
+    batches = [batch for batch in ([0], middle, far_first[:-1][:1]) if batch]
+    once = 1 + lax.div(me, n)
+    turn = 0
+    for batch in batches:
+        @pl.loop(0, once)
+        def arrive(_, batch=batch):
+            for group in batch:
+                expected = members - 1 if isinstance(group, int) else members
+                wait_ids(group, expected)
+                wait_rows(recv1, expected, arrive_sem.at[group])
+
+        if batch is batches[-1]:
+            peak, mass = normalizers()
+        rank_groups(turn, batch)
+        turn += len(batch)
+    for batch in reversed(batches):
+        for group in batch:
+            finish(group, peak, mass)
+            give_back(group)
     own_back = pltpu.make_async_copy(
         send2.at[pl.ds(member_me, 1)], recv2.at[pl.ds(me, 1)], own_sem.at[2]
     )
@@ -394,7 +433,7 @@
         width = query.shape[1]
         hidden_width = w_first.shape[1]
         message = width + hidden_width
-        tall = round_up((width + hidden_width) // LANES, 8)
+        tall = round_up((width + hidden_width) // LANES, 8) + 1
         vmem = pl.BlockSpec(memory_space=pltpu.VMEM)
         groups = math.gcd(4, item_size)
         section, weight = pl.pallas_call(
@@ -427,7 +466,7 @@
                 pltpu.SemaphoreType.DMA((groups,)),
                 pltpu.SemaphoreType.DMA,
                 pltpu.SemaphoreType.DMA((3,)),
-                pltpu.VMEM((item_table.shape[0], tall, LANES), F32),
+                pltpu.VMEM((item_table.shape[0] * tall, LANES), F32),
                 pltpu.VMEM((n * cap * tall + tall, LANES), F32),
                 pltpu.SMEM((n, 1, LANES), jnp.int32),
             ],

time: 25.5 us -> 24.1 us (0.945)
  Pallas kernels: 21 us -> 19.6 us
    pallas_call x1, Pallas kernels: 21 us -> 19.6 us  [body(): pl.pallas_call(functools.partial(kernel, dp_size, item_size, groups, cap)...]
where the time goes in v3:
time: 24.1 us; the launch traced here: 23.9 us
  Pallas kernels  19.6 us (81%)
  between operations  3.74 us (16%)
  local copies, waits for them, and re-layouts  0.6 us (2%)
    pallas_call x1, Pallas kernels, body(): pl.pallas_call(functools.partial(kernel, dp_size, item_size, groups, cap)...  19.6 us
    unnamed x1, local copies, waits for them, and re-layouts  0.6 us

profile of v3, /device:TPU:0, one launch (start us, length us, event | category | flops | bytes accessed | tf_op | source)
XLA Modules:
  0.0 23.9 jit_solution(4855922814350400803)
XLA Ops:
  2.6 19.6 %propensity.1 = (f32[1,1024]{1,0:T(1,128)S(1)}, f32[1,1]{1,0:T(1,128)S(1)}) custom-call(bf16[1,256]{1,0:T(2,128)(2,1)} %query_hbm.1, bf16[1,512]{1,0:T(2,128)(2,1)} %feature_hbm.1, s32[1,1024]{1,0:T(1,128)} %cand_hbm.1, s32[1]{0:T(128)S(6)} %copy.16.length_hbm, s32[1]{0:T(128)S(6)} %copy.17.slot_hbm, s32[1]{0:T(128)S(6)} %copy.18.prop_hbm, ...), custom_call_target="tpu_custom_call" | custom-call | tf_op jit(solution)/shard_map/propensity/pallas_call | solution.py:439
  22.2 0.6 %copy.14 = f32[1,1024]{1,0:T(1,128)} copy(f32[1,1024]{1,0:T(1,128)S(1)} %get-tuple-element.6) | data formatting | bytes 8192

commit v4 on v3

--- a/solution.py
+++ b/solution.py
@@ -102,18 +102,33 @@
     def greet(member, peer, where):
         pl.semaphore_signal(barrier, inc=1, device_id=where, device_id_type=pl.DeviceIdType.MESH)
 
-    end = jnp.where(2 * run_me < groups, groups - 1, 0)
-    far = lax.rem(end - run_me + groups, groups)
-    middle = [jnp.where(far <= k, k + 1, k) for k in range(1, groups - 1)]
-    far_first = ([far] if groups > 1 else []) + middle[::-1] + [0]
+    def farthest(plane):
+        end = jnp.where(2 * plane < groups, groups - 1, 0)
+        return lax.rem(end - plane + groups, groups)
+
+    def turn_at(plane, offset):
+        far = farthest(plane)
+        place = offset - 1 - jnp.where(offset > far, 1, 0)
+        place = jnp.where(2 * plane < groups, groups - 3 - place, place)
+        return jnp.where(offset == far, 1, 2 + place)
+
+    far = farthest(run_me)
+    rising = [jnp.where(far <= k, k + 1, k) for k in range(1, groups - 1)]
+    middle = [
+        jnp.where(2 * run_me < groups, down, up) for up, down in zip(rising, rising[::-1])
+    ]
+    offsets = [0] + ([far] if groups > 1 else []) + middle
+    far_first = offsets[1:] + [0]
+
+    cand_load = pltpu.make_async_copy(cand_hbm, cand_ref, load_sem.at[0])
+    cand_load.start()
     for offset in far_first:
         each_peer(offset, greet)
 
     loads = [
-        pltpu.make_async_copy(source, target, load_sem.at[i])
+        pltpu.make_async_copy(source, target, load_sem.at[i + 1])
         for i, (source, target) in enumerate(
             [
-                (cand_hbm, cand_ref),
                 (query_hbm, query_ref),
                 (feature_hbm, feature_ref),
                 (first_hbm, first),
@@ -128,7 +143,7 @@
     ]
     for load in loads:
         load.start()
-    loads[0].wait()
+    cand_load.wait()
 
     ids = cand_ref[...]
     holder = lax.div(ids, item_rows)
@@ -167,19 +182,18 @@
     scale = tall
     send_ids[:, 0, :] = jnp.clip(asked, 0, item_rows - 1) * scale
 
-    for load in loads[1:4]:
+    for load in loads[:3]:
         load.wait()
     context_part = dot(feature_ref[...], first[:feature_width, :], NN) * 0.5
     send1[0, :, :width] = query_ref[...].astype(F32)
     send1[0, :, width:] = context_part
-    for load in loads[4:]:
+    for load in loads[3:]:
         load.wait()
-    second_w[...] = second_w[...] * jnp.asarray(0.5, BF16)
 
     hidden_tiles = hidden_width // LANES
     step = math.gcd(256, item_rows)
     strips = item_rows // step
-    early = lax.div(strips * jnp.maximum(groups - 2 * run_me, 0), groups)
+    early = lax.div(strips * jnp.maximum(groups - 2 * run_me, 0), 2 * groups)
 
     def project(start, stop):
         @pl.loop(start, stop)
@@ -201,7 +215,11 @@
     pl.semaphore_wait(barrier, n - 1)
 
     def ask(offset):
-        seen = lax.rem(groups - offset, groups)
+        if isinstance(offset, int):
+            seen = 0
+        else:
+            plane = lax.rem(run_me + offset, groups)
+            seen = turn_at(plane, groups - offset)
 
         def act(member, peer, where):
             slot = pl.ds(seen * members + member_me, 1)
@@ -224,24 +242,18 @@
 
         each_peer(offset, act)
 
-    def give_back(group):
-        offset = group
-
-        @pl.loop(0, members)
-        def visit(j):
-            member = lax.rem(member_me + j, members)
-            peer, where = device(offset, member)
-
-            @pl.when(peer != me)
-            def send():
-                pltpu.make_async_remote_copy(
-                    src_ref=send2.at[pl.ds(offset * members + member, 1)],
-                    dst_ref=recv2.at[pl.ds(me, 1)],
-                    send_sem=send_sem.at[1],
-                    recv_sem=return_sem,
-                    device_id=where,
-                    device_id_type=pl.DeviceIdType.MESH,
-                ).start()
+    def give_back(turn):
+        def act(member, peer, where):
+            pltpu.make_async_remote_copy(
+                src_ref=send2.at[pl.ds(turn * members + member, 1)],
+                dst_ref=recv2.at[pl.ds(me, 1)],
+                send_sem=send_sem.at[1],
+                recv_sem=return_sem,
+                device_id=where,
+                device_id_type=pl.DeviceIdType.MESH,
+            ).start()
+
+        each_peer(offsets[turn], act)
 
     def wait_ids(group, expected):
         rows = wanted.at[pl.ds(group * members, expected)]
@@ -253,7 +265,7 @@
         rows = buffer.at[pl.ds(0, count)]
         pltpu.make_async_copy(rows, rows, semaphore).wait()
 
-    for offset in (far_first[:1] + far_first[:0:-1]):
+    for offset in (offsets[1:2] + [0] + offsets[2:]):
         ask(offset)
     own_ids = pltpu.make_async_copy(
         send_ids.at[pl.ds(me, 1)], wanted.at[pl.ds(member_me, 1)], own_sem.at[0]
@@ -261,6 +273,7 @@
     own_ids.start()
     own_ask = pltpu.make_async_copy(send1, recv1.at[pl.ds(member_me, 1)], own_sem.at[1])
     own_ask.start()
+    second_w[...] = second_w[...] * jnp.asarray(0.5, BF16)
     project(early, strips)
     own_ids.wait()
     own_ask.wait()
@@ -347,25 +360,26 @@
         result = jnp.where(lane == max_at, own_lane(peak), send2[rows_here, 0, :])
         send2[rows_here, 0, :] = jnp.where(lane == max_at + 1, own_lane(mass), result)
 
-    batches = [batch for batch in ([0], middle, far_first[:-1][:1]) if batch]
     once = 1 + lax.div(me, n)
-    turn = 0
-    for batch in batches:
+
+    def arrive(turns):
         @pl.loop(0, once)
-        def arrive(_, batch=batch):
-            for group in batch:
-                expected = members - 1 if isinstance(group, int) else members
-                wait_ids(group, expected)
-                wait_rows(recv1, expected, arrive_sem.at[group])
-
-        if batch is batches[-1]:
-            peak, mass = normalizers()
-        rank_groups(turn, batch)
-        turn += len(batch)
-    for batch in reversed(batches):
-        for group in batch:
-            finish(group, peak, mass)
-            give_back(group)
+        def check(_):
+            for turn in turns:
+                expected = members if turn else members - 1
+                wait_ids(turn, expected)
+                wait_rows(recv1, expected, arrive_sem.at[turn])
+
+    arrive([0])
+    rank_groups(0, [0])
+    others = list(range(1, groups))
+    arrive(others)
+    peak, mass = normalizers()
+    for turn in others + [0]:
+        if turn:
+            rank_groups(turn, [turn])
+        finish(turn, peak, mass)
+        give_back(turn)
     own_back = pltpu.make_async_copy(
         send2.at[pl.ds(member_me, 1)], recv2.at[pl.ds(me, 1)], own_sem.at[2]
     )

time: 24.1 us -> 23.5 us (0.975)
  Pallas kernels: 19.6 us -> 19 us
    pallas_call x1, Pallas kernels: 19.6 us -> 19 us  [body(): pl.pallas_call(functools.partial(kernel, dp_size, item_size, groups, cap)...]
where the time goes in v4:
time: 23.5 us; the launch traced here: 23.3 us
  Pallas kernels  19 us (81%)
  between operations  3.74 us (16%)
  local copies, waits for them, and re-layouts  0.6 us (3%)
    pallas_call x1, Pallas kernels, body(): pl.pallas_call(functools.partial(kernel, dp_size, item_size, groups, cap)...  19 us
    unnamed x1, local copies, waits for them, and re-layouts  0.6 us

profile of v4, /device:TPU:0, one launch (start us, length us, event | category | flops | bytes accessed | tf_op | source)
XLA Modules:
  0.0 23.3 jit_solution(14342050461435388427)
XLA Ops:
  2.6 19.0 %propensity.1 = (f32[1,1024]{1,0:T(1,128)S(1)}, f32[1,1]{1,0:T(1,128)S(1)}) custom-call(bf16[1,256]{1,0:T(2,128)(2,1)} %query_hbm.1, bf16[1,512]{1,0:T(2,128)(2,1)} %feature_hbm.1, s32[1,1024]{1,0:T(1,128)} %cand_hbm.1, s32[1]{0:T(128)S(6)} %copy.16.length_hbm, s32[1]{0:T(128)S(6)} %copy.17.slot_hbm, s32[1]{0:T(128)S(6)} %copy.18.prop_hbm, ...), custom_call_target="tpu_custom_call" | custom-call | tf_op jit(solution)/shard_map/propensity/pallas_call | solution.py:453
  21.6 0.6 %copy.14 = f32[1,1024]{1,0:T(1,128)} copy(f32[1,1024]{1,0:T(1,128)S(1)} %get-tuple-element.6) | data formatting | bytes 8192

commit v5 on v4

--- a/solution.py
+++ b/solution.py
@@ -70,6 +70,7 @@
     items,
     found,
     wanted,
+    tile_ref,
 ):
     n = dp_size * item_size
     item_rows, width = table.shape
@@ -274,6 +275,10 @@
     own_ask = pltpu.make_async_copy(send1, recv1.at[pl.ds(member_me, 1)], own_sem.at[1])
     own_ask.start()
     second_w[...] = second_w[...] * jnp.asarray(0.5, BF16)
+    for b in range(blocks):
+        part = slice(b * LANES, (b + 1) * LANES)
+        tile_ref[0, b : b + 1] = rank[:, part].astype(jnp.int32)
+        tile_ref[1, b : b + 1] = holder[:, part]
     project(early, strips)
     own_ids.wait()
     own_ask.wait()
@@ -284,8 +289,7 @@
     split = 1 << (math.gcd(4, copies).bit_length() - 1)
     part_rows = item_rows // split
 
-    def rank_groups(turn, batch):
-        count = cap * members * len(batch)
+    def gather(turn, batch):
         base = turn * cap * members
         for r in range(cap):
             for b, group in enumerate(batch):
@@ -293,6 +297,10 @@
                     at = wanted[group * members + c, 0, r]
                     place = base + (r * len(batch) + b) * members + c
                     found[pl.ds(place * tall, lines)] = items[pl.ds(at, lines)]
+
+    def rank_groups(turn, batch):
+        count = cap * members * len(batch)
+        base = turn * cap * members
 
         def found_tile(j):
             return found[pl.ds(base * tall + j, count, stride=tall), :]
@@ -371,13 +379,18 @@
                 wait_rows(recv1, expected, arrive_sem.at[turn])
 
     arrive([0])
+    gather(0, [0])
     rank_groups(0, [0])
     others = list(range(1, groups))
     arrive(others)
+    for turn in others[:1]:
+        gather(turn, [turn])
     peak, mass = normalizers()
     for turn in others + [0]:
         if turn:
             rank_groups(turn, [turn])
+        for later in others[turn : turn + 1] if turn else []:
+            gather(later, [later])
         finish(turn, peak, mass)
         give_back(turn)
     own_back = pltpu.make_async_copy(
@@ -390,38 +403,50 @@
     wait_rows(recv2, n - 1, return_sem)
 
     back = recv2[:, 0, :]
-    top = back.astype(BF16)
-    rest = back - top.astype(F32)
-    middle = rest.astype(BF16)
-    bottom = (rest - middle.astype(F32)).astype(BF16)
-    pieces = jnp.concatenate([top.astype(F32), middle.astype(F32), bottom.astype(F32)], axis=0)
-    held_bf = held.astype(BF16)
-    spread = dot(
-        pieces.astype(BF16).T, jnp.concatenate([held_bf, held_bf, held_bf], axis=0), NN
-    )
-    score = jnp.sum(at_rank[:gen_at] * spread[:gen_at], axis=0, keepdims=True)
-    gen = jnp.sum(at_rank[:gen_at] * spread[gen_at : 2 * gen_at], axis=0, keepdims=True)
-
     maxima = back[:, max_at : max_at + 1]
     sums = back[:, max_at + 1 : max_at + 2]
     peak = jnp.max(maxima, axis=0, keepdims=True)
     log_norm = peak + jnp.log(jnp.sum(sums * jnp.exp(maxima - peak), axis=0, keepdims=True))
 
+    rank_tile, holder_tile = tile_ref[0], tile_ref[1]
+    gen_tile = rank_tile + gen_at
+    tile = (blocks, LANES)
+
+    def look_up(h, found_so_far):
+        score, gen = found_so_far
+        line = jnp.broadcast_to(recv2[h], tile)
+        here = holder_tile == h
+        score = jnp.where(here, jnp.take_along_axis(line, rank_tile, axis=1), score)
+        gen = jnp.where(here, jnp.take_along_axis(line, gen_tile, axis=1), gen)
+        return score, gen
+
+    blank = (jnp.zeros(tile, F32), jnp.zeros(tile, F32))
+    if n <= 64:
+        score, gen = functools.reduce(lambda value, h: look_up(h, value), range(n), blank)
+    else:
+        score, gen = lax.fori_loop(0, n, look_up, blank)
+
+    def whole(reduce, value):
+        return reduce(reduce(value, axis=0, keepdims=True), axis=1, keepdims=True)
+
     length = length_ref[0]
-    position = lax.broadcasted_iota(jnp.int32, (1, slots), 1)
+    position = lax.broadcasted_iota(jnp.int32, tile, 0) * LANES + lax.broadcasted_iota(
+        jnp.int32, tile, 1
+    )
     live = position < length
     masked = jnp.where(live, score, -1e30)
-    rank_peak = jnp.max(masked, axis=1, keepdims=True)
+    rank_peak = whole(jnp.max, masked)
     rank_norm = rank_peak + jnp.log(
-        jnp.sum(jnp.where(live, jnp.exp(masked - rank_peak), 0.0), axis=1, keepdims=True)
+        whole(jnp.sum, jnp.where(live, jnp.exp(masked - rank_peak), 0.0))
     )
     section = jnp.where(
         live, score - rank_norm + gen - log_norm + math.log(item_rows * n), 0.0
     )
-    chosen = jnp.sum(jnp.where(position == slot_ref[0], section, 0.0), axis=1, keepdims=True)
+    chosen = whole(jnp.sum, jnp.where(position == slot_ref[0], section, 0.0))
     count = jnp.full((1, 1), length, jnp.int32).astype(F32)
     prop = jnp.full((1, 1), prop_ref[0], jnp.int32).astype(F32) / 1024.0
-    section_ref[...] = section
+    for b in range(blocks):
+        section_ref[:, b * LANES : (b + 1) * LANES] = section[b : b + 1]
     weight_ref[...] = chosen + jnp.log(count) - jnp.log(prop)
     wait_rows(send2, n - 1, send_sem.at[1])
 
@@ -483,6 +508,7 @@
                 pltpu.VMEM((item_table.shape[0] * tall, LANES), F32),
                 pltpu.VMEM((n * cap * tall + tall, LANES), F32),
                 pltpu.SMEM((n, 1, LANES), jnp.int32),
+                pltpu.VMEM((2, slots // LANES, LANES), jnp.int32),
             ],
             compiler_params=pltpu.CompilerParams(collective_id=0, has_side_effects=True),
             name="propensity",

time: 23.5 us -> 23.2 us (0.987)
  Pallas kernels: 19 us -> 18.6 us
    pallas_call x1, Pallas kernels: 19 us -> 18.6 us  [body(): pl.pallas_call(functools.partial(kernel, dp_size, item_size, groups, cap)...]
where the time goes in v5:
time: 23.2 us; the launch traced here: 22.9 us
  Pallas kernels  18.6 us (80%)
  between operations  3.74 us (16%)
  local copies, waits for them, and re-layouts  0.6 us (3%)
    pallas_call x1, Pallas kernels, body(): pl.pallas_call(functools.partial(kernel, dp_size, item_size, groups, cap)...  18.6 us
    unnamed x1, local copies, waits for them, and re-layouts  0.6 us

profile of v5, /device:TPU:0, one launch (start us, length us, event | category | flops | bytes accessed | tf_op | source)
XLA Modules:
  0.0 22.9 jit_solution(16045176466170510270)
XLA Ops:
  2.6 18.6 %propensity.1 = (f32[1,1024]{1,0:T(1,128)S(1)}, f32[1,1]{1,0:T(1,128)S(1)}) custom-call(bf16[1,256]{1,0:T(2,128)(2,1)} %query_hbm.1, bf16[1,512]{1,0:T(2,128)(2,1)} %feature_hbm.1, s32[1,1024]{1,0:T(1,128)} %cand_hbm.1, s32[1]{0:T(128)S(6)} %copy.16.length_hbm, s32[1]{0:T(128)S(6)} %copy.17.slot_hbm, s32[1]{0:T(128)S(6)} %copy.18.prop_hbm, ...), custom_call_target="tpu_custom_call" | custom-call | tf_op jit(solution)/shard_map/propensity/pallas_call | solution.py:478
  21.2 0.6 %copy.14 = f32[1,1024]{1,0:T(1,128)} copy(f32[1,1024]{1,0:T(1,128)S(1)} %get-tuple-element.6) | data formatting | bytes 8192

commit v6 on v5

--- a/solution.py
+++ b/solution.py
@@ -45,7 +45,6 @@
     second_hbm,
     score_hbm,
     section_ref,
-    weight_ref,
     query_ref,
     feature_ref,
     cand_ref,
@@ -447,7 +446,9 @@
     prop = jnp.full((1, 1), prop_ref[0], jnp.int32).astype(F32) / 1024.0
     for b in range(blocks):
         section_ref[:, b * LANES : (b + 1) * LANES] = section[b : b + 1]
-    weight_ref[...] = chosen + jnp.log(count) - jnp.log(prop)
+    section_ref[:, slots:] = jnp.broadcast_to(
+        chosen + jnp.log(count) - jnp.log(prop), (1, LANES)
+    )
     wait_rows(send2, n - 1, send_sem.at[1])
 
 
@@ -475,14 +476,13 @@
         tall = round_up((width + hidden_width) // LANES, 8) + 1
         vmem = pl.BlockSpec(memory_space=pltpu.VMEM)
         groups = math.gcd(4, item_size)
-        section, weight = pl.pallas_call(
+        (packed,) = pl.pallas_call(
             functools.partial(kernel, dp_size, item_size, groups, cap),
             out_shape=(
-                pltpu.VMEM((1, slots), F32),
-                pltpu.VMEM((1, 1), F32),
+                pltpu.VMEM((1, slots + LANES), F32),
             ),
             in_specs=[pl.BlockSpec(memory_space=pltpu.HBM)] * 10,
-            out_specs=(vmem, vmem),
+            out_specs=(vmem,),
             scratch_shapes=[
                 pltpu.VMEM(query.shape, BF16),
                 pltpu.VMEM(context_features.shape, BF16),
@@ -524,7 +524,7 @@
             w_second,
             w_score,
         )
-        return section, weight.reshape(-1)
+        return packed[:, :slots], packed[0, slots : slots + 1]
 
     split = P(("dp", "item"))
     rows = P(("dp", "item"), None)

time: 23.2 us -> 22.5 us (0.970)
  between operations: 3.74 us -> 2.58 us
  local copies, waits for them, and re-layouts: 0.6 us -> 1.11 us
    slice x0 -> x2, local copies, waits for them, and re-layouts: none -> 1.11 us  [body(): return (packed[:, :slots], packed[0, slots:slots + 1])]
    unnamed x1 -> x0, local copies, waits for them, and re-layouts: 0.6 us -> none
where the time goes in v6:
time: 22.5 us; the launch traced here: 22.3 us
  Pallas kernels  18.6 us (83%)
  between operations  2.58 us (11%)
  local copies, waits for them, and re-layouts  1.11 us (5%)
    pallas_call x1, Pallas kernels, body(): pl.pallas_call(functools.partial(kernel, dp_size, item_size, groups, cap)...  18.6 us
    slice x2, local copies, waits for them, and re-layouts, body(): return (packed[:, :slots], packed[0, slots:slots + 1])  1.11 us

profile of v6, /device:TPU:0, one launch (start us, length us, event | category | flops | bytes accessed | tf_op | source)
XLA Modules:
  0.0 22.3 jit_solution(14090671929287452173)
XLA Ops:
  2.6 18.6 %propensity.1 = f32[1,1152]{1,0:T(1,128)S(1)} custom-call(bf16[1,256]{1,0:T(2,128)(2,1)} %query_hbm.1, bf16[1,512]{1,0:T(2,128)(2,1)} %feature_hbm.1, s32[1,1024]{1,0:T(1,128)} %cand_hbm.1, s32[1]{0:T(128)S(6)} %copy.12.length_hbm, s32[1]{0:T(128)S(6)} %copy.13.slot_hbm, s32[1]{0:T(128)S(6)} %copy.14.prop_hbm, bf16[2048,256]{1,0:T(8,128)(2,1)} %table_hbm.1, ...), custom_call_target="tpu_custom_call" | custom-call | tf_op jit(solution)/shard_map/propensity/pallas_call | solution.py:479
  21.2 0.5 %slice.7 = f32[1,1]{1,0:T(1,128)} slice(f32[1,1152]{1,0:T(1,128)S(1)} %propensity.1), slice={[0:1], [1024:1025]} | slice | bytes 8 | tf_op jit(solution)/shard_map/slice | solution.py:527
  21.7 0.6 %slice.6 = f32[1,1024]{1,0:T(1,128)} slice(f32[1,1152]{1,0:T(1,128)S(1)} %propensity.1), slice={[0:1], [0:1024]} | slice | bytes 8192 | tf_op jit(solution)/shard_map/slice | solution.py:527
